TPU v7x, 32 devices: a whole 2x2x4 slice. The times are simulated.
32 devices in a mesh: row: 8 (over z, y), col: 4 (over x, core).
Axes of the slice: x: 2, y: 2, z: 4, core: 2. Of those that a mesh axis runs over, the one named last changes fastest.
Arguments:
- image_states: bfloat16 [64, 3072], P(('row', 'col')), may hold values from -6 to 6
- latent: float32 [64, 64], P(('row', 'col')), may hold values from -6 to 6
- text_keys: bfloat16 [1024, 3072], P('row', 'col')
- text_values: bfloat16 [1024, 3072], P('row', 'col'), may hold values from -6 to 6
- mod_table: float32 [4, 8, 3072], replicated, may hold values from -3 to 3
- timestep: int32 [4], replicated, may hold values from 0 to 3
- grid_size: int32 [4, 2], replicated, may hold values from 1 to 8, as said below
- rope_offset: int32 [4, 2], replicated, may hold values from 0 to 63
- w_qkv: bfloat16 [3072, 9216], P(None, 'row'), may hold values from -0.109375 to 0.109375
- q_gain: float32 [128], replicated, may hold values from 0.1 to 1.9
- k_gain: float32 [128], replicated, may hold values from 0.5 to 4
- w_out: bfloat16 [3072, 3072], P('col', 'row'), may hold values from -0.109375 to 0.109375
- w_fc1: bfloat16 [3072, 12288], P(None, 'row'), may hold values from -0.109375 to 0.109375
- w_fc2: bfloat16 [12288, 3072], P('row'), may hold values from -0.0546875 to 0.0546875
- w_final: bfloat16 [3072, 64], replicated, may hold values from -0.109375 to 0.109375
Outputs:
- velocity: float32 [64, 64], P(('row', 'col'))
- next_latent: float32 [64, 64], P(('row', 'col'))
Inputs may be any that keep to these rules, and one draw needn't show every extreme that they name: `grid_size`: column 0 is a request's grid height, at most 2; column 1 its grid width, at most 8; in every draw some request has height 2 and some request width 8.
All inputs are finite; a program needn't handle non-finite values.
Results may differ from a plain program's by a relative error of at most 0.008.
Values may be sent and summed in bfloat16 or wider, within the bound.
No kernel may reach another device: no remote copies, remote signals or barrier semaphores. Data moves between devices by JAX's collectives and lax.ppermute only.
A program may use at most 128 MiB of HBM per device.

v0:
```python
import jax
import jax.numpy as jnp
from jax import lax
from jax.sharding import PartitionSpec as P

REQ = 4
TXT = 256
STEPS = 4
eps_norm = 1e-06
blend = 0.25
mask_floor = -1e30


def with_halo(cells, sides, width):
    for axis, dim in sides:
        count = lax.axis_size(axis)
        ends = count - 1
        head = lax.slice_in_dim(cells, 0, width, axis=dim)
        tail = lax.slice_in_dim(cells, cells.shape[dim] - width, cells.shape[dim], axis=dim)
        cells = jnp.concatenate(
            [
                lax.ppermute(tail, axis, [(i, (i + 1) % count) for i in range(ends)]),
                cells,
                lax.ppermute(head, axis, [((i + 1) % count, i) for i in range(ends)]),
            ],
            axis=dim,
        )
    return cells


def layer_norm(values):
    mean_value = jnp.mean(values, -1, keepdims=True)
    centred = values - mean_value
    return centred * lax.rsqrt(jnp.mean(centred * centred, -1, keepdims=True) + eps_norm)


def modulate(values, shift_vec, scale_vec):
    return (layer_norm(values) * (1.0 + scale_vec) + shift_vec).astype(jnp.bfloat16)


def rope_tables(pos_h, pos_w, head_size):
    time_half = head_size // 16
    axis_dim = (head_size - head_size // 8) // 2
    freq_index = jnp.arange(axis_dim // 2, dtype=jnp.float32)
    frequency = 10000.0 ** (-2.0 * freq_index / axis_dim)
    angles = jnp.concatenate(
        [
            jnp.zeros((pos_h.shape[0], time_half), jnp.float32),
            pos_h[:, None] * frequency[None, :],
            pos_w[:, None] * frequency[None, :],
        ],
        1,
    )
    return (jnp.cos(angles), jnp.sin(angles))


def norm_rope(values, gain_vec, cosine_table, sine_table, head_count, head_size):
    row_total = values.shape[0]
    per_head = values.astype(jnp.float32).reshape(row_total, head_count, head_size)
    per_head = (
        per_head * lax.rsqrt(jnp.mean(per_head * per_head, -1, keepdims=True) + eps_norm) * gain_vec
    )
    paired = per_head.reshape(row_total, head_count, head_size // 2, 2)
    even_part = paired[..., 0]
    odd_part = paired[..., 1]
    cos_wide = cosine_table[:, None, :]
    sin_wide = sine_table[:, None, :]
    turned = jnp.stack(
        [even_part * cos_wide - odd_part * sin_wide, even_part * sin_wide + odd_part * cos_wide], -1
    )
    return turned.reshape(row_total, head_count * head_size).astype(jnp.bfloat16)


def on_device(
    image_states,
    latent,
    text_keys,
    text_values,
    mod_table,
    timestep,
    grid_size,
    rope_offset,
    w_qkv,
    q_gain,
    k_gain,
    w_out,
    w_fc1,
    w_fc2,
    w_final,
):
    col_total = lax.axis_size("col")
    row_pos = lax.axis_index("row")
    col_pos = lax.axis_index("col")
    tile_w = image_states.shape[0]
    width = image_states.shape[1]
    head_size = q_gain.shape[0]
    head_count = width // head_size
    local_heads = head_count // col_total
    request = row_pos % REQ
    grid_row = row_pos // REQ
    grid_col = col_pos * tile_w + jnp.arange(tile_w, dtype=jnp.int32)
    req_slots = jnp.arange(REQ, dtype=jnp.int32)
    req_onehot = req_slots == request
    limits = jnp.sum(jnp.where(req_onehot[:, None], grid_size, 0), 0)
    offsets = jnp.sum(jnp.where(req_onehot[:, None], rope_offset, 0), 0)
    step_now = jnp.sum(jnp.where(req_onehot, timestep, 0))
    token_ok = (grid_row < limits[0]) & (grid_col < limits[1])
    modulation = lax.dynamic_index_in_dim(mod_table, step_now, 0, keepdims=False)
    states = image_states.astype(jnp.float32)
    normed = modulate(states, modulation[0], modulation[1])
    joined_cols = jnp.dot(
        lax.all_gather(normed, "row", axis=0, tiled=True), w_qkv, preferred_element_type=jnp.float32
    ).astype(jnp.bfloat16)
    joined = lax.all_to_all(joined_cols, "row", split_axis=0, concat_axis=1, tiled=True)
    pos_h = jnp.zeros((tile_w,), jnp.float32) + (grid_row + offsets[0]).astype(jnp.float32)
    pos_w = (grid_col + offsets[1]).astype(jnp.float32)
    cosine_table, sine_table = rope_tables(pos_h, pos_w, head_size)
    queries = norm_rope(joined[:, :width], q_gain, cosine_table, sine_table, head_count, head_size)
    image_keys = norm_rope(
        joined[:, width : 2 * width], k_gain, cosine_table, sine_table, head_count, head_size
    )
    q_heads, k_heads, v_heads = (
        lax.all_to_all(queries, "col", split_axis=1, concat_axis=0, tiled=True),
        lax.all_to_all(image_keys, "col", split_axis=1, concat_axis=0, tiled=True),
        lax.all_to_all(joined[:, 2 * width :], "col", split_axis=1, concat_axis=0, tiled=True),
    )
    image_rows = k_heads.shape[0]
    text_rows = text_keys.shape[0]
    shard_rows = image_rows + text_rows
    q_block = q_heads.reshape(image_rows, local_heads, head_size)
    key_rows = jnp.concatenate([k_heads, text_keys], 0)
    value_rows = jnp.concatenate([v_heads, text_values], 0)
    run_max = jnp.full((image_rows, local_heads), mask_floor, jnp.float32)
    key_piece = lax.all_gather(key_rows, "row", axis=0, tiled=True)
    value_piece = lax.all_gather(value_rows, "row", axis=0, tiled=True)
    piece_rows = key_piece.shape[0]
    global_row = jnp.arange(piece_rows, dtype=jnp.int32)
    shard_id = global_row // shard_rows
    within = global_row % shard_rows
    is_image = within < image_rows
    source_col = within // tile_w
    source_cell = within % tile_w
    image_req = shard_id % REQ
    text_req = (shard_id * text_rows + within - image_rows) // TXT
    key_req = jnp.where(is_image, image_req, text_req)
    key_onehot = key_req[:, None] == req_slots[None, :]
    key_height = jnp.sum(jnp.where(key_onehot, grid_size[:, 0][None, :], 0), 1)
    key_width = jnp.sum(jnp.where(key_onehot, grid_size[:, 1][None, :], 0), 1)
    image_ok = (shard_id // REQ < key_height) & (source_col * tile_w + source_cell < key_width)
    key_ok = (key_req == request) & (jnp.logical_not(is_image) | image_ok)
    scores = jnp.einsum(
        "qhd,khd->qhk",
        q_block,
        key_piece.reshape(piece_rows, local_heads, head_size),
        preferred_element_type=jnp.float32,
    ) * head_size ** (-0.5)
    new_max = jnp.maximum(run_max, jnp.max(jnp.where(key_ok, scores, mask_floor), -1))
    weights = jnp.where(key_ok, jnp.exp(scores - new_max[..., None]), 0.0)
    new_sum = jnp.sum(weights, -1)
    new_acc = jnp.einsum(
        "qhk,khd->qhd",
        weights.astype(jnp.bfloat16),
        value_piece.reshape(piece_rows, local_heads, head_size),
        preferred_element_type=jnp.float32,
    )
    mixed = (
        (new_acc / new_sum[..., None])
        .astype(jnp.bfloat16)
        .reshape(image_rows, local_heads * head_size)
    )
    partial_out = jnp.dot(
        mixed, lax.all_gather(w_out, "row", axis=1, tiled=True), preferred_element_type=jnp.float32
    )
    attended = lax.psum_scatter(
        partial_out.astype(jnp.bfloat16), "col", scatter_dimension=0, tiled=True
    ).astype(jnp.float32)
    first_res = (states + modulation[2] * attended).astype(jnp.bfloat16)
    normed_two = modulate(first_res.astype(jnp.float32), modulation[3], modulation[4])
    all_rows = lax.all_gather(normed_two, "row", axis=0, tiled=True)
    hidden = jax.nn.gelu(
        jnp.dot(all_rows, w_fc1, preferred_element_type=jnp.float32), approximate=True
    ).astype(jnp.bfloat16)
    every_term = jnp.dot(hidden, w_fc2, preferred_element_type=jnp.float32)
    every_sum = lax.psum(every_term, "row")
    mlp_out = lax.dynamic_slice_in_dim(every_sum, row_pos * tile_w, tile_w, 0)
    second_res = first_res.astype(jnp.float32) + modulation[5] * mlp_out
    normed_three = modulate(second_res, modulation[6], modulation[7])
    raw_velocity = jnp.dot(normed_three, w_final, preferred_element_type=jnp.float32)
    masked = jnp.where(token_ok[:, None], raw_velocity, 0.0)
    padded = with_halo(masked, (("col", 0),), 1)
    left_side = padded[:-2]
    right_side = padded[2:]
    velocity = jnp.where(
        token_ok[:, None], masked + blend * (left_side + right_side - 2.0 * masked), 0.0
    )
    next_latent = latent + -1.0 / STEPS * velocity
    return (velocity, next_latent)


def solution(mesh):
    placed = (
        P(("row", "col"), None),
        P(("row", "col"), None),
        P("row", "col"),
        P("row", "col"),
        P(),
        P(),
        P(),
        P(),
        P(None, "row"),
        P(),
        P(),
        P("col", "row"),
        P(None, "row"),
        P("row", None),
        P(),
    )
    return jax.shard_map(
        on_device,
        mesh=mesh,
        in_specs=placed,
        out_specs=(P(("row", "col"), None), P(("row", "col"), None)),
        check_vma=False,
    )
```

profile of v0, /device:TPU:1, one launch (start us, length us, event | category | flops | bytes accessed | tf_op | source)
XLA Modules:
  0.0 413.6 jit_solution(1863781639350607465)
XLA Ops:
  15.3 25.6 %all-gather = bf16[8,2,3072]{2,1,0:T(2,128)(2,1)S(1)} all-gather(bf16[1,2,3072]{2,1,0:T(2,128)(2,1)S(1)} %fusion.50), channel_id=1, replica_groups=mesh['row'=8,'col'=4] {'row'}, dimensions={0}, use_global_device_ids=true | all-gather | bytes 110592 | tf_op jit(solution)/shard_map/all_gather | solution.py:112
  41.0 4.0 convolution_convert_fusion.1
  45.7 5.0 %all-to-all-start = ((bf16[8,2,1152]{2,1,0:T(2,128)(2,1)}), bf16[8,2,1152]{2,1,0:T(2,128)(2,1)S(1)}, u32[]{:S(2)}, u32[]{:S(2)}) async-start(bf16[8,2,1152]{2,1,0:T(2,128)(2,1)} %all_to_all.50), calls=%async_computation | async-start | bytes 73728 | tf_op jit(solution)/shard_map/all_to_all | solution.py:114
  63.3 5.2 %slice_multiply_fusion.5 = (f32[2,24,64,1]{3,2,1,0:T(8,128)}, f32[2,24,64,1]{3,2,1,0:T(8,128)}, f32[2,24,64,1]{3,2,1,0:T(8,128)}, f32[2,24,64,1]{3,2,1,0:T(8,128...) fusion(f32[2,24,64,2]{3,2,1,0:T(8,128)S(1)} %multiply_multiply_, ...), kind=kLoop, calls=%fused_computation.11 | loop fusion | flops 24576 | bytes 148480 | tf_op jit(solution)/shard_map/mul | solution.py:69
  68.5 2.5 copy.52
  73.6 2.5 copy.54
  76.1 2.5 copy.55
  84.9 14.5 %all_to_all.67 = bf16[2,4,768]{2,0,1:T(2,128)(2,1)} all-to-all(bf16[2,4,768]{2,0,1:T(2,128)(2,1)S(1)} %copy.57), channel_id=1, replica_groups=mesh['row'=8,'col'=4] {'col'}, dimensions={1} | all-to-all | bytes 24576 | tf_op jit(solution)/shard_map/all_to_all | solution.py:124
  101.8 7.8 %all_to_all.68 = bf16[2,4,768]{2,0,1:T(2,128)(2,1)} all-to-all(bf16[2,4,768]{2,0,1:T(2,128)(2,1)} %bitcast.72), channel_id=1, replica_groups=mesh['row'=8,'col'=4] {'col'}, dimensions={1} | all-to-all | bytes 24576 | tf_op jit(solution)/shard_map/all_to_all | solution.py:125
  112.8 2.5 copy.59
  115.4 2.5 copy.60
  121.9 3.9 all-to-all-start.3
  129.4 14.7 %all-gather.8.cloned.1.call-done = bf16[1088,768]{1,0:T(8,128)(2,1)} async-done(((bf16[136,768]{1,0:T(8,128)(2,1)}), bf16[1088,768]{1,0:T(8,128)(2,1)}) %all-gather.8.cloned.1.call-update) | async-done | bytes 1671184 | tf_op jit(solution)/shard_map/all_gather | solution.py:134
  144.1 3.8 copy.58
  147.9 42.3 %all-gather.6.cloned.1.call-done = bf16[1088,768]{1,0:T(8,128)(2,1)} async-done(((bf16[136,768]{1,0:T(8,128)(2,1)}), bf16[1088,768]{1,0:T(8,128)(2,1)}) %all-gather.6.cloned.1.call-update) | async-done | bytes 1671184 | tf_op jit(solution)/shard_map/all_gather | solution.py:135
  190.2 2.7 copy.51
  195.0 77.3 %all-gather.10.cloned.1.call-done = bf16[768,3072]{1,0:T(8,128)(2,1)} async-done(((bf16[768,384]{1,0:T(8,128)(2,1)}), bf16[768,3072]{1,0:T(8,128)(2,1)}) %all-gather.10.cloned.1.call-update) | async-done | bytes 4718608 | tf_op jit(solution)/shard_map/all_gather | solution.py:172
  272.3 3.7 convolution_convert_fusion
  276.0 11.2 %all-reduce = bf16[8,3072]{1,0:T(8,128)(2,1)S(1)} all-reduce(bf16[8,3072]{1,0:T(8,128)(2,1)S(1)} %convolution_convert_fusion), channel_id=2, replica_groups=mesh['row'=8,'col'=4] {'col'}, use_global_device_ids=true, to_apply=%region_11.12.clone | all-reduce | flops 24576 | bytes 98304
  287.7 24.4 %all-gather.1 = bf16[8,2,3072]{2,1,0:T(2,128)(2,1)S(1)} all-gather(bf16[1,2,3072]{2,1,0:T(2,128)(2,1)S(1)} %fusion.51), channel_id=1, replica_groups=mesh['row'=8,'col'=4] {'row'}, dimensions={0}, use_global_device_ids=true | all-gather | bytes 110592 | tf_op jit(solution)/shard_map/all_gather | solution.py:179
  312.2 9.6 %fusion.22 = f32[16,3072]{1,0:T(8,128)} fusion(bf16[1536,3072]{1,0:T(8,128)(2,1)} %param.28, bf16[16,3072]{1,0:T(8,128)(2,1)S(1)} %reshape.272, bf16[3072,1536]{1,0:T(8,128)(2,1)} %param.27), kind=kOutput, calls=%fused_computation.37 | convolution fusion | flops 302211072 | bytes 19169280 | tf_op jit(solution)/shard_map/dot_general | solution.py:183
  323.0 71.4 %all-reduce.3.cloned.1.call-done = f32[16,3072]{1,0:T(8,128)} async-done(((f32[16,3072]{1,0:T(8,128)}), f32[16,3072]{1,0:T(8,128)}) %all-reduce.3.cloned.1.call-update) | async-done | bytes 196624 | tf_op jit(solution)/shard_map/psum | solution.py:184
  396.0 5.6 %collective-permute-start = (f32[1,64]{1,0:T(1,128)S(1)}, f32[1,64]{1,0:T(1,128)S(1)}, u32[]{:S(2)}, u32[]{:S(2)}) collective-permute-start(f32[1,64]{1,0:T(1,128)S(1)} %get-tuple-element.45), channel_id=1, source_target_pairs={{0,1},{1,2},{2,3},{4,5},{5,6},{6,7},{8,9},{9,10},{10,11},{12,13},{... | collective-permute-start | bytes 776 | tf_op jit(solution)/shard_map/ppermute | solution.py:22
  403.5 2.9 collective-permute-done.1
  (121 shorter events, 47.4 us)
Async XLA Ops:
  7.2 388.5 %copy-start = (bf16[3072,64]{0,1:T(8,128)(2,1)S(1)}, bf16[3072,64]{0,1:T(8,128)(2,1)}, u32[]{:S(2)}) copy-start(bf16[3072,64]{0,1:T(8,128)(2,1)} %param.29) | copy-start | bytes 1179652
  41.0 9.8 %copy-start.12 = (s32[4,2]{0,1:T(2,128)S(1)}, s32[4,2]{0,1:T(2,128)}, u32[]{:S(2)}) copy-start(s32[4,2]{0,1:T(2,128)} %param.21) | copy-start | bytes 100
  41.0 9.8 %copy-start.13 = (s32[4,2]{0,1:T(2,128)S(1)}, s32[4,2]{0,1:T(2,128)}, u32[]{:S(2)}) copy-start(s32[4,2]{0,1:T(2,128)} %param.22) | copy-start | bytes 100
  41.0 12.1 %copy-start.15 = (f32[128]{0:T(128)S(1)}, f32[128]{0:T(128)}, u32[]{:S(2)}) copy-start(f32[128]{0:T(128)} %param.24) | copy-start | bytes 1540
  41.0 12.9 %copy-start.16 = (f32[128]{0:T(128)S(1)}, f32[128]{0:T(128)}, u32[]{:S(2)}) copy-start(f32[128]{0:T(128)} %param.25) | copy-start | bytes 1540
  45.7 10.6 %all-to-all-start = ((bf16[8,2,1152]{2,1,0:T(2,128)(2,1)}), bf16[8,2,1152]{2,1,0:T(2,128)(2,1)S(1)}, u32[]{:S(2)}, u32[]{:S(2)}) async-start(bf16[8,2,1152]{2,1,0:T(2,128)(2,1)} %all_to_all.50), calls=%async_computation | async-start | bytes 73728 | tf_op jit(solution)/shard_map/all_to_all | solution.py:114
  50.7 93.4 %all-gather.8.cloned.1.call-start = ((), (), s32[]{:S(2)}) async-start(), calls=%async_computation.5 | async-start | bytes 1880064 | tf_op jit(solution)/shard_map/all_gather | solution.py:134
  62.2 1.0 copy-start.2
  101.8 88.4 %all-gather.6.cloned.1.call-start = ((), (), s32[]{:S(2)}) async-start(), calls=%async_computation.4 | async-start | bytes 1880064 | tf_op jit(solution)/shard_map/all_gather | solution.py:135
  111.9 160.4 %all-gather.10.cloned.1.call-start = ((), (), s32[]{:S(2)}) async-start(), calls=%async_computation.6 | async-start | bytes 5308416 | tf_op jit(solution)/shard_map/all_gather | solution.py:172
  119.0 0.8 copy-start.5
  119.0 6.9 %copy-start.17 = (u32[32]{0:T(128)S(1)}, u32[32]{0:T(128)}, u32[]{:S(2)}) copy-start(u32[32]{0:T(128)} %constant.158) | copy-start | bytes 388
  121.9 7.5 %all-to-all-start.3 = ((bf16[2,4,768]{2,0,1:T(2,128)(2,1)}), bf16[2,4,768]{2,0,1:T(2,128)(2,1)S(1)}, u32[]{:S(2)}, u32[]{:S(2)}) async-start(bf16[2,4,768]{2,0,1:T(2,128)(2,1)} %copy.64), calls=%async_computation.3 | async-start | bytes 24576 | tf_op jit(solution)/shard_map/all_to_all | solution.py:123
  125.9 268.5 %all-reduce.3.cloned.1.call-start = ((), (), s32[]{:S(2)}) async-start(), calls=%async_computation.7 | async-start | bytes 393216 | tf_op jit(solution)/shard_map/psum | solution.py:184
  272.3 14.9 %copy-start.1 = (bf16[2,3072]{1,0:T(2,128)(2,1)S(1)}, bf16[2,3072]{1,0:T(2,128)(2,1)}, u32[]{:S(2)}) copy-start(bf16[2,3072]{1,0:T(2,128)(2,1)} %param.15) | copy-start | bytes 36868
  272.3 14.9 %copy-start.9 = (f32[1,1,3072]{2,1,0:T(1,128)S(1)}, f32[1,1,3072]{2,1,0:T(1,128)}, u32[]{:S(2)}) copy-start(f32[1,1,3072]{2,1,0:T(1,128)} %get-tuple-element.30) | copy-start | bytes 36868
  272.3 15.3 %copy-start.7 = (f32[1,1,3072]{2,1,0:T(1,128)S(1)}, f32[1,1,3072]{2,1,0:T(1,128)}, u32[]{:S(2)}) copy-start(f32[1,1,3072]{2,1,0:T(1,128)} %get-tuple-element.25) | copy-start | bytes 36868
  272.3 15.3 %copy-start.8 = (f32[1,1,3072]{2,1,0:T(1,128)S(1)}, f32[1,1,3072]{2,1,0:T(1,128)}, u32[]{:S(2)}) copy-start(f32[1,1,3072]{2,1,0:T(1,128)} %get-tuple-element.26) | copy-start | bytes 36868
  312.1 82.3 %copy-start.6 = (f32[1,1,3072]{2,1,0:T(1,128)S(1)}, f32[1,1,3072]{2,1,0:T(1,128)}, u32[]{:S(2)}) copy-start(f32[1,1,3072]{2,1,0:T(1,128)} %get-tuple-element.27) | copy-start | bytes 36868
  312.1 83.6 %copy-start.10 = (f32[1,1,3072]{2,1,0:T(1,128)S(1)}, f32[1,1,3072]{2,1,0:T(1,128)}, u32[]{:S(2)}) copy-start(f32[1,1,3072]{2,1,0:T(1,128)} %get-tuple-element.24) | copy-start | bytes 36868
  312.1 83.6 %copy-start.11 = (f32[1,1,3072]{2,1,0:T(1,128)S(1)}, f32[1,1,3072]{2,1,0:T(1,128)}, u32[]{:S(2)}) copy-start(f32[1,1,3072]{2,1,0:T(1,128)} %get-tuple-element.31) | copy-start | bytes 36868
  312.1 94.3 %copy-start.14 = (f32[2,64]{1,0:T(2,128)S(1)}, f32[2,64]{1,0:T(2,128)}, u32[]{:S(2)}) copy-start(f32[2,64]{1,0:T(2,128)} %param.16) | copy-start | bytes 1540
  396.0 7.5 %collective-permute-start = (f32[1,64]{1,0:T(1,128)S(1)}, f32[1,64]{1,0:T(1,128)S(1)}, u32[]{:S(2)}, u32[]{:S(2)}) collective-permute-start(f32[1,64]{1,0:T(1,128)S(1)} %get-tuple-element.45), channel_id=1, source_target_pairs={{0,1},{1,2},{2,3},{4,5},{5,6},{6,7},{8,9},{9,10},{10,11},{12,13},{... | collective-permute-start | bytes 776 | tf_op jit(solution)/shard_map/ppermute | solution.py:22
  401.5 4.9 %collective-permute-start.1 = (f32[1,64]{1,0:T(1,128)S(1)}, f32[1,64]{1,0:T(1,128)S(1)}, u32[]{:S(2)}, u32[]{:S(2)}) collective-permute-start(f32[1,64]{1,0:T(1,128)S(1)} %get-tuple-element.46), channel_id=1, source_target_pairs={{1,0},{2,1},{3,2},{5,4},{6,5},{7,6},{9,8},{10,9},{11,10},{13,12},{... | collective-permute-start | bytes 776 | tf_op jit(solution)/shard_map/ppermute | solution.py:24
  (2 other events, 1.5 us)
Sparse Core Ops, SparseCore 0:
  101.9 42.1 all-gather.7
  146.3 43.8 all-gather.5
  192.3 79.9 all-gather.9
  321.9 72.4 all-reduce.2
where the time goes:
time: 415 us; the launch traced here: 414 us
  waiting for transfers between devices  213 us (51%)
  blocking collectives  83.5 us (20%)
  local copies, waits for them, and re-layouts  38.6 us (9%)
  other arithmetic  24.4 us (6%)
  matrix products  19.5 us (5%)
  between operations  18 us (4%)
  starting transfers between devices  16.5 us (4%)
    all_gather x1, waiting for transfers between devices, on_device(): lax.all_gather(w_out, 'row', axis=1, tiled=True)  77.3 us
    psum x1, waiting for transfers between devices, on_device(): every_sum = lax.psum(every_term, 'row')  71.4 us
    all_gather x1, waiting for transfers between devices, on_device(): value_piece = lax.all_gather(value_rows, 'row', axis=0, tiled=True)  42.3 us
    all_gather x1, blocking collectives, on_device(): lax.all_gather(normed, 'row', axis=0, tiled=True)  25.6 us
    all_gather x1, blocking collectives, on_device(): all_rows = lax.all_gather(normed_two, 'row', axis=0, tiled=True)  24.4 us
    all_gather x1, waiting for transfers between devices, on_device(): key_piece = lax.all_gather(key_rows, 'row', axis=0, tiled=True)  14.7 us
    all_to_all x1, blocking collectives, on_device(): lax.all_to_all(image_keys, 'col', split_axis=1, concat_axis=0, tiled=True)  14.5 us
    unnamed x1, blocking collectives  11.2 us
  transfers between devices with their start and end apart: 8, of which 7 were waited for; matrix products, arithmetic and copies ran while one was open for 6% of the time, Pallas kernels for 0%

commit v1 on v0

--- a/solution.py
+++ b/solution.py
@@ -132,7 +132,12 @@
     value_rows = jnp.concatenate([v_heads, text_values], 0)
     run_max = jnp.full((image_rows, local_heads), mask_floor, jnp.float32)
     key_piece = lax.all_gather(key_rows, "row", axis=0, tiled=True)
-    value_piece = lax.all_gather(value_rows, "row", axis=0, tiled=True)
+    ring = [value_rows]
+    for hop in range(7):
+        ring.append(lax.ppermute(ring[-1], "row", [(dev, (dev + 1) % 8) for dev in range(8)]))
+    value_piece = jnp.roll(
+        jnp.concatenate(ring[::-1], axis=0), (lax.axis_index("row") + 1) * ring[0].shape[0], axis=0
+    )
     piece_rows = key_piece.shape[0]
     global_row = jnp.arange(piece_rows, dtype=jnp.int32)
     shard_id = global_row // shard_rows

time: 415 us -> 388 us (0.935)
  waiting for transfers between devices: 213 us -> 162 us
  starting transfers between devices: 16.5 us -> 30.5 us
  local copies, waits for them, and re-layouts: 38.6 us -> 45.5 us
    ppermute x0 -> x7, waiting for transfers between devices: none -> 50.2 us  [on_device(): lax.ppermute(ring[-1], 'row', [(dev, (dev + 1) % 8) for dev in range(8)])]
    all_gather x1, waiting for transfers between devices: 77.3 us -> 33.2 us  [on_device(): lax.all_gather(w_out, 'row', axis=1, tiled=True)]
    all_gather x1 -> x0, waiting for transfers between devices: 42.3 us -> none  [on_device(): value_piece = lax.all_gather(value_rows, 'row', axis=0, tiled=True)]
    all_gather x1, waiting for transfers between devices: 14.7 us -> 0.02 us  [on_device(): key_piece = lax.all_gather(key_rows, 'row', axis=0, tiled=True)]
    all_to_all x1, starting transfers between devices: 3.94 us -> 17.7 us  [on_device(): lax.all_to_all(queries, 'col', split_axis=1, concat_axis=0, tiled=True)]
    unnamed x39 -> x62, local copies, waits for them, and re-layouts: 0.96 us -> 6.11 us
    dynamic_slice x0 -> x2, local copies, waits for them, and re-layouts: none -> 4.36 us  [on_device(): jnp.roll(jnp.concatenate(ring[::-1], axis=0), (lax.axis_index('row') + 1)...]
  transfers between devices with their start and end apart: 8 -> 14, of which waited for: 7 -> 11; matrix products, arithmetic and copies ran while one was open for 6% -> 8% of each run, Pallas kernels for 0% -> 0%
where the time goes in v1:
time: 388 us; the launch traced here: 386 us
  waiting for transfers between devices  162 us (42%)
  blocking collectives  83.5 us (22%)
  local copies, waits for them, and re-layouts  45.5 us (12%)
  starting transfers between devices  30.5 us (8%)
  other arithmetic  26.6 us (7%)
  matrix products  19.5 us (5%)
  between operations  18.3 us (5%)
    psum x1, waiting for transfers between devices, on_device(): every_sum = lax.psum(every_term, 'row')  71.3 us
    ppermute x7, waiting for transfers between devices, on_device(): lax.ppermute(ring[-1], 'row', [(dev, (dev + 1) % 8) for dev in range(8)])  50.2 us
    all_gather x1, waiting for transfers between devices, on_device(): lax.all_gather(w_out, 'row', axis=1, tiled=True)  33.2 us
    all_gather x1, blocking collectives, on_device(): lax.all_gather(normed, 'row', axis=0, tiled=True)  25.6 us
    all_gather x1, blocking collectives, on_device(): all_rows = lax.all_gather(normed_two, 'row', axis=0, tiled=True)  24.4 us
    all_to_all x1, starting transfers between devices, on_device(): lax.all_to_all(queries, 'col', split_axis=1, concat_axis=0, tiled=True)  17.7 us
    all_to_all x1, blocking collectives, on_device(): lax.all_to_all(image_keys, 'col', split_axis=1, concat_axis=0, tiled=True)  14.5 us
    unnamed x1, blocking collectives  11.2 us
  transfers between devices with their start and end apart: 14, of which 11 were waited for; matrix products, arithmetic and copies ran while one was open for 8% of the time, Pallas kernels for 0%

profile of v1, /device:TPU:1, one launch (start us, length us, event | category | flops | bytes accessed | tf_op | source)
XLA Modules:
  0.0 385.9 jit_solution(3877132394213461064)
XLA Ops:
  15.3 25.6 %all-gather = bf16[8,2,3072]{2,1,0:T(2,128)(2,1)S(1)} all-gather(bf16[1,2,3072]{2,1,0:T(2,128)(2,1)S(1)} %fusion.50), channel_id=1, replica_groups=mesh['row'=8,'col'=4] {'row'}, dimensions={0}, use_global_device_ids=true | all-gather | bytes 110592 | tf_op jit(solution)/shard_map/all_gather | solution.py:112
  41.0 4.0 %convolution_convert_fusion.1 = bf16[16,1152]{1,0:T(8,128)(2,1)S(1)} fusion(bf16[16,3072]{1,0:T(8,128)(2,1)S(1)} %reshape.270, bf16[3072,1152]{1,0:T(8,128)(2,1)} %param.23), kind=kOutput, calls=%fused_computation.3 | convolution fusion | flops 113264640 | bytes 7213056 | tf_op jit(solution)/shard_map/dot_general | solution.py:111
  45.7 5.0 %all-to-all-start = ((bf16[8,2,1152]{2,1,0:T(2,128)(2,1)}), bf16[8,2,1152]{2,1,0:T(2,128)(2,1)S(1)}, u32[]{:S(2)}, u32[]{:S(2)}) async-start(bf16[8,2,1152]{2,1,0:T(2,128)(2,1)} %all_to_all.50), calls=%async_computation | async-start | bytes 73728 | tf_op jit(solution)/shard_map/all_to_all | solution.py:114
  64.1 5.2 %slice_multiply_fusion.5 = (f32[2,24,64,1]{3,2,1,0:T(8,128)}, f32[2,24,64,1]{3,2,1,0:T(8,128)}, f32[2,24,64,1]{3,2,1,0:T(8,128)}, f32[2,24,64,1]{3,2,1,0:T(8,128...) fusion(f32[2,24,64,2]{3,2,1,0:T(8,128)S(1)} %multiply_multiply_, ...), kind=kLoop, calls=%fused_computation.11 | loop fusion | flops 24576 | bytes 148480 | tf_op jit(solution)/shard_map/mul | solution.py:69
  69.3 2.5 copy.54
  85.7 14.5 %all_to_all.67 = bf16[2,4,768]{2,0,1:T(2,128)(2,1)} all-to-all(bf16[2,4,768]{2,0,1:T(2,128)(2,1)S(1)} %copy.57), channel_id=1, replica_groups=mesh['row'=8,'col'=4] {'col'}, dimensions={1} | all-to-all | bytes 24576 | tf_op jit(solution)/shard_map/all_to_all | solution.py:124
  103.4 7.7 %all_to_all.68 = bf16[2,4,768]{2,0,1:T(2,128)(2,1)} all-to-all(bf16[2,4,768]{2,0,1:T(2,128)(2,1)} %bitcast.72), channel_id=1, replica_groups=mesh['row'=8,'col'=4] {'col'}, dimensions={1} | all-to-all | bytes 24576 | tf_op jit(solution)/shard_map/all_to_all | solution.py:125
  113.0 12.5 %collective-permute-done = bf16[136,768]{1,0:T(8,128)(2,1)S(1)} collective-permute-done((bf16[136,768]{1,0:T(8,128)(2,1)S(1)}, bf16[136,768]{1,0:T(8,128)(2,1)S(1)}, u32[]{:S(2)}, u32[]{:S(2)}) %collective-permute-start) | collective-permute-done | bytes 208928 | tf_op jit(solution)/shard_map/ppermute | solution.py:137
  126.2 9.7 %collective-permute-done.1 = bf16[136,768]{1,0:T(8,128)(2,1)S(1)} collective-permute-done((bf16[136,768]{1,0:T(8,128)(2,1)S(1)}, bf16[136,768]{1,0:T(8,128)(2,1)S(1)}, u32[]{:S(2)}, u32[]{:S(2)}) %collective-permute-start.1) | collective-permute-done | bytes 208928 | tf_op jit(solution)/shard_map/ppermute | solution.py:137
  136.6 12.0 %collective-permute-done.2 = bf16[136,768]{1,0:T(8,128)(2,1)} collective-permute-done((bf16[136,768]{1,0:T(8,128)(2,1)S(1)}, bf16[136,768]{1,0:T(8,128)(2,1)}, u32[]{:S(2)}, u32[]{:S(2)}) %collective-permute-start.2) | collective-permute-done | bytes 208928 | tf_op jit(solution)/shard_map/ppermute | solution.py:137
  151.8 2.5 copy.62
  157.0 7.6 %collective-permute-done.4 = bf16[136,768]{1,0:T(8,128)(2,1)S(1)} collective-permute-done((bf16[136,768]{1,0:T(8,128)(2,1)}, bf16[136,768]{1,0:T(8,128)(2,1)S(1)}, u32[]{:S(2)}, u32[]{:S(2)}) %collective-permute-start.4) | collective-permute-done | bytes 208928 | tf_op jit(solution)/shard_map/ppermute | solution.py:137
  167.4 17.7 %all-to-all-start.3 = ((bf16[2,4,768]{2,0,1:T(2,128)(2,1)}), bf16[2,4,768]{2,0,1:T(2,128)(2,1)S(1)}, u32[]{:S(2)}, u32[]{:S(2)}) async-start(bf16[2,4,768]{2,0,1:T(2,128)(2,1)} %copy.64), calls=%async_computation.3 | async-start | bytes 24576 | tf_op jit(solution)/shard_map/all_to_all | solution.py:123
  188.6 8.3 %collective-permute-done.6 = bf16[136,768]{1,0:T(8,128)(2,1)S(1)} collective-permute-done((bf16[136,768]{1,0:T(8,128)(2,1)S(1)}, bf16[136,768]{1,0:T(8,128)(2,1)S(1)}, u32[]{:S(2)}, u32[]{:S(2)}) %collective-permute-start.6) | collective-permute-done | bytes 208928 | tf_op jit(solution)/shard_map/ppermute | solution.py:137
  202.6 2.7 copy.51
  205.4 3.9 %copy.58 = bf16[1088,768]{0,1:T(8,128)(2,1)} copy(bf16[1088,768]{1,0:T(8,128)(2,1)} %all-gather.5.cloned.1.call-done) | data formatting | bytes 3342336 | tf_op jit(solution)/shard_map/all_gather | solution.py:134
  211.4 33.2 %all-gather.7.cloned.1.call-done = bf16[768,3072]{1,0:T(8,128)(2,1)} async-done(((bf16[768,384]{1,0:T(8,128)(2,1)}), bf16[768,3072]{1,0:T(8,128)(2,1)}) %all-gather.7.cloned.1.call-update) | async-done | bytes 4718608 | tf_op jit(solution)/shard_map/all_gather | solution.py:177
  244.6 3.7 convolution_convert_fusion
  248.2 11.2 %all-reduce = bf16[8,3072]{1,0:T(8,128)(2,1)S(1)} all-reduce(bf16[8,3072]{1,0:T(8,128)(2,1)S(1)} %convolution_convert_fusion), channel_id=2, replica_groups=mesh['row'=8,'col'=4] {'col'}, use_global_device_ids=true, to_apply=%region_11.12.clone | all-reduce | flops 24576 | bytes 98304
  259.9 24.4 %all-gather.1 = bf16[8,2,3072]{2,1,0:T(2,128)(2,1)S(1)} all-gather(bf16[1,2,3072]{2,1,0:T(2,128)(2,1)S(1)} %fusion.51), channel_id=1, replica_groups=mesh['row'=8,'col'=4] {'row'}, dimensions={0}, use_global_device_ids=true | all-gather | bytes 110592 | tf_op jit(solution)/shard_map/all_gather | solution.py:184
  284.4 9.6 %fusion.22 = f32[16,3072]{1,0:T(8,128)} fusion(bf16[1536,3072]{1,0:T(8,128)(2,1)} %param.28, bf16[16,3072]{1,0:T(8,128)(2,1)S(1)} %reshape.272, bf16[3072,1536]{1,0:T(8,128)(2,1)} %param.27), kind=kOutput, calls=%fused_computation.37 | convolution fusion | flops 302211072 | bytes 19169280 | tf_op jit(solution)/shard_map/dot_general | solution.py:188
  295.4 71.3 %all-reduce.3.cloned.1.call-done = f32[16,3072]{1,0:T(8,128)} async-done(((f32[16,3072]{1,0:T(8,128)}), f32[16,3072]{1,0:T(8,128)}) %all-reduce.3.cloned.1.call-update) | async-done | bytes 196624 | tf_op jit(solution)/shard_map/psum | solution.py:189
  368.3 5.6 %collective-permute-start.7 = (f32[1,64]{1,0:T(1,128)S(1)}, f32[1,64]{1,0:T(1,128)S(1)}, u32[]{:S(2)}, u32[]{:S(2)}) collective-permute-start(f32[1,64]{1,0:T(1,128)S(1)} %get-tuple-element.45), channel_id=1, source_target_pairs={{0,1},{1,2},{2,3},{4,5},{5,6},{6,7},{8,9},{9,10},{10,11},{12,13},{... | collective-permute-start | bytes 776 | tf_op jit(solution)/shard_map/ppermute | solution.py:22
  375.8 2.9 collective-permute-done.8
  (157 shorter events, 64.3 us)
Async XLA Ops:
  7.2 360.8 %copy-start = (bf16[3072,64]{0,1:T(8,128)(2,1)S(1)}, bf16[3072,64]{0,1:T(8,128)(2,1)}, u32[]{:S(2)}) copy-start(bf16[3072,64]{0,1:T(8,128)(2,1)} %param.29) | copy-start | bytes 1179652
  45.7 10.6 %all-to-all-start = ((bf16[8,2,1152]{2,1,0:T(2,128)(2,1)}), bf16[8,2,1152]{2,1,0:T(2,128)(2,1)S(1)}, u32[]{:S(2)}, u32[]{:S(2)}) async-start(bf16[8,2,1152]{2,1,0:T(2,128)(2,1)} %all_to_all.50), calls=%async_computation | async-start | bytes 73728 | tf_op jit(solution)/shard_map/all_to_all | solution.py:114
  50.7 154.7 %all-gather.5.cloned.1.call-start = ((), (), s32[]{:S(2)}) async-start(), calls=%async_computation.4 | async-start | bytes 1880064 | tf_op jit(solution)/shard_map/all_gather | solution.py:134
  102.6 142.0 %all-gather.7.cloned.1.call-start = ((), (), s32[]{:S(2)}) async-start(), calls=%async_computation.5 | async-start | bytes 5308416 | tf_op jit(solution)/shard_map/all_gather | solution.py:177
  112.8 12.7 %collective-permute-start = (bf16[136,768]{1,0:T(8,128)(2,1)S(1)}, bf16[136,768]{1,0:T(8,128)(2,1)S(1)}, u32[]{:S(2)}, u32[]{:S(2)}) collective-permute-start(bf16[136,768]{1,0:T(8,128)(2,1)S(1)} %pad_maximum_fusion), channel_id=1, source_target_pairs={{0,4},{4,8},{8,12},{12,16},{16,20},{20,24},{24,28},{28,0},{1,5},{5... | collective-permute-start | bytes 626696 | tf_op jit(solution)/shard_map/ppermute | solution.py:137
  126.2 9.7 %collective-permute-start.1 = (bf16[136,768]{1,0:T(8,128)(2,1)S(1)}, bf16[136,768]{1,0:T(8,128)(2,1)S(1)}, u32[]{:S(2)}, u32[]{:S(2)}) collective-permute-start(bf16[136,768]{1,0:T(8,128)(2,1)S(1)} %collective-permute-done), channel_id=1, source_target_pairs={{0,4},{4,8},{8,12},{12,16},{16,20},{20,24},{24,28},{28,0},{1,5},{5... | collective-permute-start | bytes 626696 | tf_op jit(solution)/shard_map/ppermute | solution.py:137
  136.6 12.0 %collective-permute-start.2 = (bf16[136,768]{1,0:T(8,128)(2,1)S(1)}, bf16[136,768]{1,0:T(8,128)(2,1)}, u32[]{:S(2)}, u32[]{:S(2)}) collective-permute-start(bf16[136,768]{1,0:T(8,128)(2,1)S(1)} %collective-permute-done.1), channel_id=1, source_target_pairs={{0,4},{4,8},{8,12},{12,16},{16,20},{20,24},{24,28},{28,0},{1,5},{5... | collective-permute-start | bytes 626696 | tf_op jit(solution)/shard_map/ppermute | solution.py:137
  148.5 7.7 %collective-permute-start.3 = (bf16[136,768]{1,0:T(8,128)(2,1)}, bf16[136,768]{1,0:T(8,128)(2,1)}, u32[]{:S(2)}, u32[]{:S(2)}) collective-permute-start(bf16[136,768]{1,0:T(8,128)(2,1)} %collective-permute-done.2), channel_id=1, source_target_pairs={{0,4},{4,8},{8,12},{12,16},{16,20},{20,24},{24,28},{28,0},{1,5},{5... | collective-permute-start | bytes 626696 | tf_op jit(solution)/shard_map/ppermute | solution.py:137
  151.8 33.4 %copy-start.20 = (u32[32]{0:T(128)S(1)}, u32[32]{0:T(128)}, u32[]{:S(2)}) copy-start(u32[32]{0:T(128)} %constant.177) | copy-start | bytes 388
  155.4 29.7 %copy-start.12 = (s32[1088]{0:T(1024)S(1)}, s32[1088]{0:T(1024)}, u32[]{:S(2)}) copy-start(s32[1088]{0:T(1024)} %get-tuple-element.3) | copy-start | bytes 13060
  155.5 43.4 %copy-start.5 = (bf16[136,768]{1,0:T(8,128)(2,1)S(1)}, bf16[136,768]{1,0:T(8,128)(2,1)}, u32[]{:S(2)}) copy-start(bf16[136,768]{1,0:T(8,128)(2,1)} %copy-done.4) | copy-start | bytes 626692
  155.5 43.4 %copy-start.3 = (bf16[136,768]{1,0:T(8,128)(2,1)S(1)}, bf16[136,768]{1,0:T(8,128)(2,1)}, u32[]{:S(2)}) copy-start(bf16[136,768]{1,0:T(8,128)(2,1)} %copy-done.2) | copy-start | bytes 626692
  155.5 43.5 %copy-start.1 = (bf16[128,768]{1,0:T(8,128)(2,1)S(1)}, bf16[128,768]{1,0:T(8,128)(2,1)}, u32[]{:S(2)}) copy-start(bf16[128,768]{1,0:T(8,128)(2,1)} %param.18) | copy-start | bytes 589828
  156.2 8.3 %collective-permute-start.4 = (bf16[136,768]{1,0:T(8,128)(2,1)}, bf16[136,768]{1,0:T(8,128)(2,1)S(1)}, u32[]{:S(2)}, u32[]{:S(2)}) collective-permute-start(bf16[136,768]{1,0:T(8,128)(2,1)} %collective-permute-done.3), channel_id=1, source_target_pairs={{0,4},{4,8},{8,12},{12,16},{16,20},{20,24},{24,28},{28,0},{1,5},{5... | collective-permute-start | bytes 626696 | tf_op jit(solution)/shard_map/ppermute | solution.py:137
  164.5 20.6 %collective-permute-start.5 = (bf16[136,768]{1,0:T(8,128)(2,1)S(1)}, bf16[136,768]{1,0:T(8,128)(2,1)S(1)}, u32[]{:S(2)}, u32[]{:S(2)}) collective-permute-start(bf16[136,768]{1,0:T(8,128)(2,1)S(1)} %collective-permute-done.4), channel_id=1, source_target_pairs={{0,4},{4,8},{8,12},{12,16},{16,20},{20,24},{24,28},{28,0},{1,5},{5... | collective-permute-start | bytes 626696 | tf_op jit(solution)/shard_map/ppermute | solution.py:137
  167.4 21.2 %all-to-all-start.3 = ((bf16[2,4,768]{2,0,1:T(2,128)(2,1)}), bf16[2,4,768]{2,0,1:T(2,128)(2,1)S(1)}, u32[]{:S(2)}, u32[]{:S(2)}) async-start(bf16[2,4,768]{2,0,1:T(2,128)(2,1)} %copy.64), calls=%async_computation.3 | async-start | bytes 24576 | tf_op jit(solution)/shard_map/all_to_all | solution.py:123
  185.1 181.6 %all-reduce.3.cloned.1.call-start = ((), (), s32[]{:S(2)}) async-start(), calls=%async_computation.6 | async-start | bytes 393216 | tf_op jit(solution)/shard_map/psum | solution.py:189
  185.1 11.8 %collective-permute-start.6 = (bf16[136,768]{1,0:T(8,128)(2,1)S(1)}, bf16[136,768]{1,0:T(8,128)(2,1)S(1)}, u32[]{:S(2)}, u32[]{:S(2)}) collective-permute-start(bf16[136,768]{1,0:T(8,128)(2,1)S(1)} %collective-permute-done.5), channel_id=1, source_target_pairs={{0,4},{4,8},{8,12},{12,16},{16,20},{20,24},{24,28},{28,0},{1,5},{5... | collective-permute-start | bytes 626696 | tf_op jit(solution)/shard_map/ppermute | solution.py:137
  284.4 82.3 %copy-start.7 = (f32[1,1,3072]{2,1,0:T(1,128)S(1)}, f32[1,1,3072]{2,1,0:T(1,128)}, u32[]{:S(2)}) copy-start(f32[1,1,3072]{2,1,0:T(1,128)} %get-tuple-element.27) | copy-start | bytes 36868
  284.4 83.6 %copy-start.13 = (f32[1,1,3072]{2,1,0:T(1,128)S(1)}, f32[1,1,3072]{2,1,0:T(1,128)}, u32[]{:S(2)}) copy-start(f32[1,1,3072]{2,1,0:T(1,128)} %get-tuple-element.24) | copy-start | bytes 36868
  284.4 83.6 %copy-start.14 = (f32[1,1,3072]{2,1,0:T(1,128)S(1)}, f32[1,1,3072]{2,1,0:T(1,128)}, u32[]{:S(2)}) copy-start(f32[1,1,3072]{2,1,0:T(1,128)} %get-tuple-element.31) | copy-start | bytes 36868
  284.4 94.3 %copy-start.17 = (f32[2,64]{1,0:T(2,128)S(1)}, f32[2,64]{1,0:T(2,128)}, u32[]{:S(2)}) copy-start(f32[2,64]{1,0:T(2,128)} %param.16) | copy-start | bytes 1540
  368.3 7.5 %collective-permute-start.7 = (f32[1,64]{1,0:T(1,128)S(1)}, f32[1,64]{1,0:T(1,128)S(1)}, u32[]{:S(2)}, u32[]{:S(2)}) collective-permute-start(f32[1,64]{1,0:T(1,128)S(1)} %get-tuple-element.45), channel_id=1, source_target_pairs={{0,1},{1,2},{2,3},{4,5},{5,6},{6,7},{8,9},{9,10},{10,11},{12,13},{... | collective-permute-start | bytes 776 | tf_op jit(solution)/shard_map/ppermute | solution.py:22
  373.8 4.9 %collective-permute-start.8 = (f32[1,64]{1,0:T(1,128)S(1)}, f32[1,64]{1,0:T(1,128)S(1)}, u32[]{:S(2)}, u32[]{:S(2)}) collective-permute-start(f32[1,64]{1,0:T(1,128)S(1)} %get-tuple-element.46), channel_id=1, source_target_pairs={{1,0},{2,1},{3,2},{5,4},{6,5},{7,6},{9,8},{10,9},{11,10},{13,12},{... | collective-permute-start | bytes 776 | tf_op jit(solution)/shard_map/ppermute | solution.py:24
  (11 other events, 136.1 us)
Sparse Core Ops, SparseCore 0:
  102.7 49.8 all-gather.4
  154.7 89.8 all-gather.6
  294.2 72.4 all-reduce.2
